TPU v7x, 32 devices: a whole 2x2x4 slice. The times are simulated.
32 devices in a mesh: node: 8 (over z, x), rep: 4 (over y, core).
Axes of the slice: x: 2, y: 2, z: 4, core: 2. Of those that a mesh axis runs over, the one named last changes fastest.
Arguments:
- features: bfloat16 [8192, 512], P(('node', 'rep')), may hold values from -6 to 6
- weight: bfloat16 [512, 512], replicated, may hold values from -0.25 to 0.25
- cotangent: bfloat16 [8192, 512], P(('node', 'rep')), may hold values from -6 to 6
- tile_values: bfloat16 [8192, 128, 128], P(('node', 'rep')), may hold values from -0.125 to 0.125
- tile_row: int32 [8192], P(('node', 'rep')), may hold values from 0 to 7
- tile_col: int32 [8192], P(('node', 'rep')), may hold values from 0 to 15
- tile_count: int32 [32], P(('node', 'rep')), may hold values from 64 to 256, as said below
Outputs:
- activation: bfloat16 [8192, 512], P(('node', 'rep'))
- weight_grad: float32 [512, 512], replicated
- feature_grad: bfloat16 [8192, 512], P(('node', 'rep'))
Inputs may be any that keep to these rules, and one draw needn't show every extreme that they name: `tile_count`: slots of a device below its count hold tiles, the others are ignored; some device uses all 256 slots.
All inputs are finite; a program needn't handle non-finite values.
Results may differ from a plain program's by a relative error of at most 0.023.
Values may be sent and summed in bfloat16 or wider, within the bound.
A program may use at most 128 MiB of HBM per device.

v0:
```python
import math
import jax
import jax.numpy as jnp
from jax import lax
from jax.sharding import PartitionSpec as P

TB = 128


def smooth_gate(values):
    return jax.nn.gelu(values, approximate=True)


def apply_tiles(
    tile_values, tile_row, tile_col, tile_count, sources, target_shape, backward, window_start
):
    group_size = min(32, tile_row.shape[0])
    filled = tile_count[0]
    turns_needed = (filled + group_size - 1) // group_size
    window_blocks = target_shape[0]

    def one_turn(turn_index, totals):
        offset = turn_index * group_size
        values = lax.dynamic_slice_in_dim(tile_values, offset, group_size, 0)
        rows_here = lax.dynamic_slice_in_dim(tile_row, offset, group_size, 0)
        cols_here = lax.dynamic_slice_in_dim(tile_col, offset, group_size, 0)
        slot_mask = (offset + jnp.arange(group_size, dtype=jnp.int32) < filled).astype(jnp.float32)
        if backward:
            local_cols = cols_here - window_start
            inside = ((local_cols >= 0) & (local_cols < window_blocks)).astype(jnp.float32)
            placed = jnp.clip(local_cols, 0, window_blocks - 1)
            product = jnp.einsum(
                "tji,tjf->tif", values, sources[rows_here], preferred_element_type=jnp.float32
            )
            return totals.at[placed].add(product * (slot_mask * inside)[:, None, None])
        product = jnp.einsum(
            "tij,tjf->tif", values, sources[cols_here], preferred_element_type=jnp.float32
        )
        return totals.at[rows_here].add(product * slot_mask[:, None, None])

    return lax.fori_loop(0, turns_needed, one_turn, jnp.zeros(target_shape, jnp.float32))


def local(features, weight, cotangent, tile_values, tile_row, tile_col, tile_count):
    rows_quarter = features.shape[0]
    feature_width = features.shape[1]
    rep_count = lax.axis_size("rep")
    node_count = lax.axis_size("node")
    scale = 1.0 / math.sqrt(rows_quarter * rep_count * node_count)
    gathered = lax.all_gather(features, "node", axis=0, tiled=True)
    source_blocks = gathered.reshape(-1, TB, feature_width)
    block_count = rows_quarter * rep_count // TB
    partial_value = apply_tiles(
        tile_values,
        tile_row,
        tile_col,
        tile_count,
        source_blocks,
        (block_count, TB, feature_width),
        False,
        0,
    ).reshape(block_count * TB, feature_width)
    aggregate_all = lax.psum(partial_value, "rep").astype(jnp.bfloat16)
    cotangent_all = lax.all_gather(cotangent, "rep", axis=0, tiled=True)
    pre = jnp.dot(aggregate_all, weight, preferred_element_type=jnp.float32)
    activated, pullback = jax.vjp(smooth_gate, pre)
    grad_all = pullback(cotangent_all.astype(jnp.float32))[0].astype(jnp.bfloat16)
    full_grad = jnp.dot(grad_all, weight.T, preferred_element_type=jnp.float32).astype(jnp.bfloat16)
    offset = lax.axis_index("rep") * rows_quarter
    own_aggregate = lax.dynamic_slice_in_dim(aggregate_all, offset, rows_quarter, 0)
    own_grad = lax.dynamic_slice_in_dim(grad_all, offset, rows_quarter, 0)
    weight_term = jnp.dot(own_aggregate.T, own_grad, preferred_element_type=jnp.float32)
    output_rows = lax.dynamic_slice_in_dim(activated, offset, rows_quarter, 0).astype(jnp.bfloat16)
    weight_grad = lax.psum(weight_term, ("node", "rep")) * scale
    grad_blocks = full_grad.reshape(block_count, TB, feature_width)
    contributions = apply_tiles(
        tile_values, tile_row, tile_col, tile_count, grad_blocks, source_blocks.shape, True, 0
    )
    feature_grad = lax.psum_scatter(
        contributions.reshape(-1, feature_width).astype(jnp.bfloat16),
        "node",
        scatter_dimension=0,
        tiled=True,
    )
    return (output_rows, weight_grad, feature_grad)


def solution(mesh):
    in_specs = (
        P(("node", "rep"), None),
        P(),
        P(("node", "rep"), None),
        P(("node", "rep"), None, None),
        P(("node", "rep")),
        P(("node", "rep")),
        P(("node", "rep")),
    )
    out_specs = (P(("node", "rep"), None), P(), P(("node", "rep"), None))
    return jax.shard_map(local, mesh=mesh, in_specs=in_specs, out_specs=out_specs, check_vma=False)
```

profile of v0, /device:TPU:0, one launch (start us, length us, event | category | flops | bytes accessed | tf_op | source)
XLA Modules:
  0.0 611.5 jit_solution(17007301135434615890)
XLA Ops:
  9.4 52.6 %all-gather.3.cloned.1.call-done = bf16[2048,512]{1,0:T(8,128)(2,1)} async-done(((bf16[256,512]{1,0:T(8,128)(2,1)}), bf16[2048,512]{1,0:T(8,128)(2,1)}) %all-gather.3.cloned.1.call-update) | async-done | bytes 2097168 | tf_op jit(solution)/shard_map/all_gather | solution.py:50
  62.3 95.9 %while.20 = (s32[]{:T(128)}, f32[8,128,512]{2,1,0:T(8,128)S(1)}, s32[]{:T(128)}, s32[256]{0:T(256)S(1)}, bf16[256,128,128]{2,1,0:T(8,128)(2,1)}, /*index=5*/s32[...) while((s32[]{:T(128)}, f32[8,128,512]{2,1,0:T(8,128)S(1)}, ...), condition=%wide.region_2.3_spmd, body=%wide.region_0.2_spmd.sunk | while | flops 541066560 | bytes 47191344 | solution.py:41
  63.0 4.4 gather_fusion
  67.4 7.2 %broadcast_multiply_fusion.5 = f32[32,128,512]{2,1,0:T(8,128)} fusion(f32[32]{0:T(128)S(1)} %compare_convert_fusion.3, bf16[32,128,512]{2,1,0:T(8,128)(2,1)} %gather_fusion, bf16[256,128,128]{2,1,0:T(8,128)(2,1)} %get-tuple-element.274, s32[]{:T(128)S(6)} %select_n.44), kind=kOutput, calls=%fused_computation.4.clone.1 | convolution fusion | flops 538968064 | bytes 13631620 | tf_op jit(solution)/shard_map/while/body/tij,tjf->tif/dot_general | solution.py:36
  74.6 11.8 %scatter_fusion = f32[8,128,512]{2,1,0:T(8,128)S(1)} fusion(f32[8,128,512]{2,1,0:T(8,128)S(1)} %get-tuple-element.259, s32[32]{0:T(128)S(1)} %get-tuple-element.234, f32[32,128,512]{2,1,0:T(8,128)} %broadcast_multiply_fusion.5), kind=kCustom, calls=%fused_computation.2.clone.1 | custom fusion | flops 2097152 | bytes 25165952 | tf_op jit(solution)/shard_map/while/body/scatter-add | solution.py:39
  87.2 4.4 gather_fusion
  91.5 7.0 %broadcast_multiply_fusion.5 = f32[32,128,512]{2,1,0:T(8,128)} fusion(f32[32]{0:T(128)S(1)} %compare_convert_fusion.3, bf16[32,128,512]{2,1,0:T(8,128)(2,1)} %gather_fusion, bf16[256,128,128]{2,1,0:T(8,128)(2,1)} %get-tuple-element.274, s32[]{:T(128)S(6)} %select_n.44), kind=kOutput, calls=%fused_computation.4.clone.1 | convolution fusion | flops 538968064 | bytes 13631620 | tf_op jit(solution)/shard_map/while/body/tij,tjf->tif/dot_general | solution.py:36
  98.5 11.8 %scatter_fusion = f32[8,128,512]{2,1,0:T(8,128)S(1)} fusion(f32[8,128,512]{2,1,0:T(8,128)S(1)} %get-tuple-element.259, s32[32]{0:T(128)S(1)} %get-tuple-element.234, f32[32,128,512]{2,1,0:T(8,128)} %broadcast_multiply_fusion.5), kind=kCustom, calls=%fused_computation.2.clone.1 | custom fusion | flops 2097152 | bytes 25165952 | tf_op jit(solution)/shard_map/while/body/scatter-add | solution.py:39
  111.1 4.4 gather_fusion
  115.4 7.0 %broadcast_multiply_fusion.5 = f32[32,128,512]{2,1,0:T(8,128)} fusion(f32[32]{0:T(128)S(1)} %compare_convert_fusion.3, bf16[32,128,512]{2,1,0:T(8,128)(2,1)} %gather_fusion, bf16[256,128,128]{2,1,0:T(8,128)(2,1)} %get-tuple-element.274, s32[]{:T(128)S(6)} %select_n.44), kind=kOutput, calls=%fused_computation.4.clone.1 | convolution fusion | flops 538968064 | bytes 13631620 | tf_op jit(solution)/shard_map/while/body/tij,tjf->tif/dot_general | solution.py:36
  122.4 11.7 %scatter_fusion = f32[8,128,512]{2,1,0:T(8,128)S(1)} fusion(f32[8,128,512]{2,1,0:T(8,128)S(1)} %get-tuple-element.259, s32[32]{0:T(128)S(1)} %get-tuple-element.234, f32[32,128,512]{2,1,0:T(8,128)} %broadcast_multiply_fusion.5), kind=kCustom, calls=%fused_computation.2.clone.1 | custom fusion | flops 2097152 | bytes 25165952 | tf_op jit(solution)/shard_map/while/body/scatter-add | solution.py:39
  134.9 4.4 gather_fusion
  139.3 7.0 %broadcast_multiply_fusion.5 = f32[32,128,512]{2,1,0:T(8,128)} fusion(f32[32]{0:T(128)S(1)} %compare_convert_fusion.3, bf16[32,128,512]{2,1,0:T(8,128)(2,1)} %gather_fusion, bf16[256,128,128]{2,1,0:T(8,128)(2,1)} %get-tuple-element.274, s32[]{:T(128)S(6)} %select_n.44), kind=kOutput, calls=%fused_computation.4.clone.1 | convolution fusion | flops 538968064 | bytes 13631620 | tf_op jit(solution)/shard_map/while/body/tij,tjf->tif/dot_general | solution.py:36
  146.3 11.8 %scatter_fusion = f32[8,128,512]{2,1,0:T(8,128)S(1)} fusion(f32[8,128,512]{2,1,0:T(8,128)S(1)} %get-tuple-element.259, s32[32]{0:T(128)S(1)} %get-tuple-element.234, f32[32,128,512]{2,1,0:T(8,128)} %broadcast_multiply_fusion.5), kind=kCustom, calls=%fused_computation.2.clone.1 | custom fusion | flops 2097152 | bytes 25165952 | tf_op jit(solution)/shard_map/while/body/scatter-add | solution.py:39
  158.1 87.7 %all-reduce.4 = bf16[1024,512]{1,0:T(8,128)(2,1)} all-reduce(f32[1024,512]{1,0:T(8,128)S(1)} %bitcast.16), channel_id=1, replica_groups=mesh['node'=8,'rep'=4] {'rep'}, use_global_device_ids=true, to_apply=%region_3.4 | all-reduce | flops 524288 | bytes 3145728 | tf_op jit(solution)/shard_map/psum | solution.py:63
  245.8 5.3 fusion.6
  256.8 117.3 %while.21 = (s32[]{:T(128)}, f32[16,128,512]{2,1,0:T(8,128)}, s32[]{:T(128)}, s32[256]{0:T(256)S(1)}, bf16[256,128,128]{2,1,0:T(8,128)(2,1)}, /*index=5*/s32[256...) while((s32[]{:T(128)}, f32[16,128,512]{2,1,0:T(8,128)}, ...), condition=%wide.region_7.8_spmd, body=%wide.region_5.7_spmd.sunk | while | flops 541066688 | bytes 47191480 | solution.py:41
  257.6 2.8 gather_fusion.1
  260.3 7.3 %broadcast_multiply_fusion.6 = f32[32,128,512]{2,1,0:T(8,128)} fusion(f32[32]{0:T(128)S(1)} %and_select_fusion.2, bf16[32,128,512]{2,1,0:T(8,128)(2,1)} %gather_fusion.1, bf16[256,128,128]{2,1,0:T(8,128)(2,1)} %get-tuple-element.310, s32[]{:T(128)S(6)} %select_n.46), kind=kOutput, calls=%fused_computation.11.clone.1 | convolution fusion | flops 538968064 | bytes 13631620 | tf_op jit(solution)/shard_map/while/body/tji,tjf->tif/dot_general | solution.py:32
  267.6 18.4 %scatter_fusion.1 = f32[16,128,512]{2,1,0:T(8,128)} fusion(f32[16,128,512]{2,1,0:T(8,128)} %get-tuple-element.295, s32[32]{0:T(128)S(1)} %get-tuple-element.244, f32[32,128,512]{2,1,0:T(8,128)} %broadcast_multiply_fusion.6), kind=kCustom, calls=%fused_computation.3.clone.1 | custom fusion | flops 2097152 | bytes 25165952 | tf_op jit(solution)/shard_map/while/body/scatter-add | solution.py:35
  286.8 2.8 gather_fusion.1
  289.5 7.3 %broadcast_multiply_fusion.6 = f32[32,128,512]{2,1,0:T(8,128)} fusion(f32[32]{0:T(128)S(1)} %and_select_fusion.2, bf16[32,128,512]{2,1,0:T(8,128)(2,1)} %gather_fusion.1, bf16[256,128,128]{2,1,0:T(8,128)(2,1)} %get-tuple-element.310, s32[]{:T(128)S(6)} %select_n.46), kind=kOutput, calls=%fused_computation.11.clone.1 | convolution fusion | flops 538968064 | bytes 13631620 | tf_op jit(solution)/shard_map/while/body/tji,tjf->tif/dot_general | solution.py:32
  296.8 18.7 %scatter_fusion.1 = f32[16,128,512]{2,1,0:T(8,128)} fusion(f32[16,128,512]{2,1,0:T(8,128)} %get-tuple-element.295, s32[32]{0:T(128)S(1)} %get-tuple-element.244, f32[32,128,512]{2,1,0:T(8,128)} %broadcast_multiply_fusion.6), kind=kCustom, calls=%fused_computation.3.clone.1 | custom fusion | flops 2097152 | bytes 25165952 | tf_op jit(solution)/shard_map/while/body/scatter-add | solution.py:35
  316.3 2.8 gather_fusion.1
  319.0 7.3 %broadcast_multiply_fusion.6 = f32[32,128,512]{2,1,0:T(8,128)} fusion(f32[32]{0:T(128)S(1)} %and_select_fusion.2, bf16[32,128,512]{2,1,0:T(8,128)(2,1)} %gather_fusion.1, bf16[256,128,128]{2,1,0:T(8,128)(2,1)} %get-tuple-element.310, s32[]{:T(128)S(6)} %select_n.46), kind=kOutput, calls=%fused_computation.11.clone.1 | convolution fusion | flops 538968064 | bytes 13631620 | tf_op jit(solution)/shard_map/while/body/tji,tjf->tif/dot_general | solution.py:32
  326.3 18.3 %scatter_fusion.1 = f32[16,128,512]{2,1,0:T(8,128)} fusion(f32[16,128,512]{2,1,0:T(8,128)} %get-tuple-element.295, s32[32]{0:T(128)S(1)} %get-tuple-element.244, f32[32,128,512]{2,1,0:T(8,128)} %broadcast_multiply_fusion.6), kind=kCustom, calls=%fused_computation.3.clone.1 | custom fusion | flops 2097152 | bytes 25165952 | tf_op jit(solution)/shard_map/while/body/scatter-add | solution.py:35
  345.5 2.8 gather_fusion.1
  348.2 7.3 %broadcast_multiply_fusion.6 = f32[32,128,512]{2,1,0:T(8,128)} fusion(f32[32]{0:T(128)S(1)} %and_select_fusion.2, bf16[32,128,512]{2,1,0:T(8,128)(2,1)} %gather_fusion.1, bf16[256,128,128]{2,1,0:T(8,128)(2,1)} %get-tuple-element.310, s32[]{:T(128)S(6)} %select_n.46), kind=kOutput, calls=%fused_computation.11.clone.1 | convolution fusion | flops 538968064 | bytes 13631620 | tf_op jit(solution)/shard_map/while/body/tji,tjf->tif/dot_general | solution.py:32
  355.5 18.5 %scatter_fusion.1 = f32[16,128,512]{2,1,0:T(8,128)} fusion(f32[16,128,512]{2,1,0:T(8,128)} %get-tuple-element.295, s32[32]{0:T(128)S(1)} %get-tuple-element.244, f32[32,128,512]{2,1,0:T(8,128)} %broadcast_multiply_fusion.6), kind=kCustom, calls=%fused_computation.3.clone.1 | custom fusion | flops 2097152 | bytes 25165952 | tf_op jit(solution)/shard_map/while/body/scatter-add | solution.py:35
  374.1 3.8 convert_element_type.37
  379.9 49.0 %all-reduce.3.cloned.1.call-done = f32[512,512]{1,0:T(8,128)} async-done(((f32[512,512]{1,0:T(8,128)}), f32[512,512]{1,0:T(8,128)}) %all-reduce.3.cloned.1.call-update) | async-done | bytes 1048592 | tf_op jit(solution)/shard_map/psum | solution.py:74
  431.2 173.9 %reduce-scatter.2.cloned.1.call-done = bf16[256,512]{1,0:T(8,128)(2,1)} async-done(((bf16[2048,512]{1,0:T(8,128)(2,1)}), bf16[256,512]{1,0:T(8,128)(2,1)}) %reduce-scatter.2.cloned.1.call-update) | async-done | bytes 262160 | tf_op jit(solution)/shard_map/reduce_scatter | solution.py:79
  (45 shorter events, 17.8 us)
Async XLA Ops:
  7.2 238.7 %copy-start = (bf16[512,512]{1,0:T(8,128)(2,1)S(1)}, bf16[512,512]{1,0:T(8,128)(2,1)}, u32[]{:S(2)}) copy-start(bf16[512,512]{1,0:T(8,128)(2,1)} %param.12) | copy-start | bytes 1572868
  7.2 55.1 %copy-start.1 = (s32[256]{0:T(256)S(1)}, s32[256]{0:T(256)}, u32[]{:S(2)}) copy-start(s32[256]{0:T(256)} %param.16) | copy-start | bytes 3076
  7.2 55.1 %copy-start.2 = (s32[256]{0:T(256)S(1)}, s32[256]{0:T(256)}, u32[]{:S(2)}) copy-start(s32[256]{0:T(256)} %param.15) | copy-start | bytes 3076
  7.2 54.8 %all-gather.3.cloned.1.call-start = ((), (), s32[]{:S(2)}) async-start(), calls=%async_computation.1 | async-start | bytes 2359296 | tf_op jit(solution)/shard_map/all_gather | solution.py:50
  7.9 237.9 %all-gather.5.cloned.1.call-start = ((), (), s32[]{:S(2)}) async-start(), calls=%async_computation.2 | async-start | bytes 1310720 | tf_op jit(solution)/shard_map/all_gather | solution.py:64
  8.7 420.2 %all-reduce.3.cloned.1.call-start = ((), (), s32[]{:S(2)}) async-start(), calls=%async_computation.3 | async-start | bytes 2097152 | tf_op jit(solution)/shard_map/psum | solution.py:74
  254.2 350.8 %reduce-scatter.2.cloned.1.call-start = ((), (), s32[]{:S(2)}) async-start(), calls=%async_computation.4 | async-start | bytes 2359296 | tf_op jit(solution)/shard_map/reduce_scatter | solution.py:79
Sparse Core Ops, SparseCore 0:
  10.1 51.7 all-gather.2
  63.5 15.2 all-gather.4
  254.3 174.4 all-reduce.2
  432.8 172.1 reduce-scatter.1
where the time goes:
time: 614 us; the launch traced here: 612 us
  waiting for transfers between devices  277 us (45%)
  other arithmetic  135 us (22%)
  blocking collectives  87.7 us (14%)
  matrix products  65.7 us (11%)
  local copies, waits for them, and re-layouts  31.2 us (5%)
  between operations  14.5 us (2%)
    reduce_scatter x1, waiting for transfers between devices, local(): lax.psum_scatter(contributions.reshape(-1, feature_width).astype(jnp.bflo...  174 us
    psum x1, blocking collectives, local(): aggregate_all = lax.psum(partial_value, 'rep').astype(jnp.bfloat16)  87.7 us
    scatter-add x4, other arithmetic, one_turn(): return totals.at[placed].add(product * (slot_mask * inside)[:, None, None])  73.9 us
    all_gather x1, waiting for transfers between devices, local(): gathered = lax.all_gather(features, 'node', axis=0, tiled=True)  52.6 us
    psum x1, waiting for transfers between devices, local(): weight_grad = lax.psum(weight_term, ('node', 'rep')) * scale  49 us
    scatter-add x4, other arithmetic, one_turn(): return totals.at[rows_here].add(product * slot_mask[:, None, None])  47.1 us
    dot_general x4, matrix products, one_turn(): jnp.einsum('tji,tjf->tif', values, sources[rows_here], preferred_element_...  29.1 us
    dot_general x4, matrix products, one_turn(): jnp.einsum('tij,tjf->tif', values, sources[cols_here], preferred_element_...  28.2 us
  transfers between devices with their start and end apart: 4, of which 3 were waited for; matrix products, arithmetic and copies ran while one was open for 37% of the time, Pallas kernels for 0%

commit v1 on v0

--- a/solution.py
+++ b/solution.py
@@ -71,7 +71,7 @@
     own_grad = lax.dynamic_slice_in_dim(grad_all, offset, rows_quarter, 0)
     weight_term = jnp.dot(own_aggregate.T, own_grad, preferred_element_type=jnp.float32)
     output_rows = lax.dynamic_slice_in_dim(activated, offset, rows_quarter, 0).astype(jnp.bfloat16)
-    weight_grad = lax.psum(weight_term, ("node", "rep")) * scale
+    weight_grad = lax.psum(lax.psum(weight_term, "node"), "rep") * scale
     grad_blocks = full_grad.reshape(block_count, TB, feature_width)
     contributions = apply_tiles(
         tile_values, tile_row, tile_col, tile_count, grad_blocks, source_blocks.shape, True, 0

time: 614 us -> 689 us (1.12)
  waiting for transfers between devices: 277 us -> 352 us
    psum x1 -> x2, waiting for transfers between devices: 49 us -> 122 us  [local(): weight_grad = lax.psum(lax.psum(weight_term, 'node'), 'rep') * scale]
  transfers between devices with their start and end apart: 4 -> 5, of which waited for: 3 -> 3; matrix products, arithmetic and copies ran while one was open for 37% -> 33% of each run, Pallas kernels for 0% -> 0%
where the time goes in v1:
time: 689 us; the launch traced here: 686 us
  waiting for transfers between devices  352 us (51%)
  other arithmetic  135 us (20%)
  blocking collectives  87.7 us (13%)
  matrix products  65.8 us (10%)
  local copies, waits for them, and re-layouts  31.3 us (5%)
  between operations  14.5 us (2%)
    reduce_scatter x1, waiting for transfers between devices, local(): lax.psum_scatter(contributions.reshape(-1, feature_width).astype(jnp.bflo...  176 us
    psum x2, waiting for transfers between devices, local(): weight_grad = lax.psum(lax.psum(weight_term, 'node'), 'rep') * scale  122 us
    psum x1, blocking collectives, local(): aggregate_all = lax.psum(partial_value, 'rep').astype(jnp.bfloat16)  87.7 us
    scatter-add x4, other arithmetic, one_turn(): return totals.at[placed].add(product * (slot_mask * inside)[:, None, None])  73.7 us
    all_gather x1, waiting for transfers between devices, local(): gathered = lax.all_gather(features, 'node', axis=0, tiled=True)  52.6 us
    scatter-add x4, other arithmetic, one_turn(): return totals.at[rows_here].add(product * slot_mask[:, None, None])  47.1 us
    dot_general x4, matrix products, one_turn(): jnp.einsum('tji,tjf->tif', values, sources[rows_here], preferred_element_...  29.3 us
    dot_general x4, matrix products, one_turn(): jnp.einsum('tij,tjf->tif', values, sources[cols_here], preferred_element_...  28.2 us
  transfers between devices with their start and end apart: 5, of which 3 were waited for; matrix products, arithmetic and copies ran while one was open for 33% of the time, Pallas kernels for 0%

profile of v1, /device:TPU:0, one launch (start us, length us, event | category | flops | bytes accessed | tf_op | source)
XLA Modules:
  0.0 686.3 jit_solution(9550597787920115238)
XLA Ops:
  9.4 52.6 %all-gather.3.cloned.1.call-done = bf16[2048,512]{1,0:T(8,128)(2,1)} async-done(((bf16[256,512]{1,0:T(8,128)(2,1)}), bf16[2048,512]{1,0:T(8,128)(2,1)}) %all-gather.3.cloned.1.call-update) | async-done | bytes 2097168 | tf_op jit(solution)/shard_map/all_gather | solution.py:50
  62.3 95.9 %while.20 = (s32[]{:T(128)}, f32[8,128,512]{2,1,0:T(8,128)S(1)}, s32[]{:T(128)}, s32[256]{0:T(256)S(1)}, bf16[256,128,128]{2,1,0:T(8,128)(2,1)}, /*index=5*/s32[...) while((s32[]{:T(128)}, f32[8,128,512]{2,1,0:T(8,128)S(1)}, ...), condition=%wide.region_2.3_spmd, body=%wide.region_0.2_spmd.sunk | while | flops 541066560 | bytes 47191344 | solution.py:41
  63.0 4.4 gather_fusion
  67.4 7.2 %broadcast_multiply_fusion.5 = f32[32,128,512]{2,1,0:T(8,128)} fusion(f32[32]{0:T(128)S(1)} %compare_convert_fusion.3, bf16[32,128,512]{2,1,0:T(8,128)(2,1)} %gather_fusion, bf16[256,128,128]{2,1,0:T(8,128)(2,1)} %get-tuple-element.274, s32[]{:T(128)S(6)} %select_n.44), kind=kOutput, calls=%fused_computation.4.clone.1 | convolution fusion | flops 538968064 | bytes 13631620 | tf_op jit(solution)/shard_map/while/body/tij,tjf->tif/dot_general | solution.py:36
  74.6 11.8 %scatter_fusion = f32[8,128,512]{2,1,0:T(8,128)S(1)} fusion(f32[8,128,512]{2,1,0:T(8,128)S(1)} %get-tuple-element.259, s32[32]{0:T(128)S(1)} %get-tuple-element.234, f32[32,128,512]{2,1,0:T(8,128)} %broadcast_multiply_fusion.5), kind=kCustom, calls=%fused_computation.2.clone.1 | custom fusion | flops 2097152 | bytes 25165952 | tf_op jit(solution)/shard_map/while/body/scatter-add | solution.py:39
  87.2 4.4 gather_fusion
  91.5 7.0 %broadcast_multiply_fusion.5 = f32[32,128,512]{2,1,0:T(8,128)} fusion(f32[32]{0:T(128)S(1)} %compare_convert_fusion.3, bf16[32,128,512]{2,1,0:T(8,128)(2,1)} %gather_fusion, bf16[256,128,128]{2,1,0:T(8,128)(2,1)} %get-tuple-element.274, s32[]{:T(128)S(6)} %select_n.44), kind=kOutput, calls=%fused_computation.4.clone.1 | convolution fusion | flops 538968064 | bytes 13631620 | tf_op jit(solution)/shard_map/while/body/tij,tjf->tif/dot_general | solution.py:36
  98.5 11.8 %scatter_fusion = f32[8,128,512]{2,1,0:T(8,128)S(1)} fusion(f32[8,128,512]{2,1,0:T(8,128)S(1)} %get-tuple-element.259, s32[32]{0:T(128)S(1)} %get-tuple-element.234, f32[32,128,512]{2,1,0:T(8,128)} %broadcast_multiply_fusion.5), kind=kCustom, calls=%fused_computation.2.clone.1 | custom fusion | flops 2097152 | bytes 25165952 | tf_op jit(solution)/shard_map/while/body/scatter-add | solution.py:39
  111.1 4.4 gather_fusion
  115.4 7.0 %broadcast_multiply_fusion.5 = f32[32,128,512]{2,1,0:T(8,128)} fusion(f32[32]{0:T(128)S(1)} %compare_convert_fusion.3, bf16[32,128,512]{2,1,0:T(8,128)(2,1)} %gather_fusion, bf16[256,128,128]{2,1,0:T(8,128)(2,1)} %get-tuple-element.274, s32[]{:T(128)S(6)} %select_n.44), kind=kOutput, calls=%fused_computation.4.clone.1 | convolution fusion | flops 538968064 | bytes 13631620 | tf_op jit(solution)/shard_map/while/body/tij,tjf->tif/dot_general | solution.py:36
  122.4 11.7 %scatter_fusion = f32[8,128,512]{2,1,0:T(8,128)S(1)} fusion(f32[8,128,512]{2,1,0:T(8,128)S(1)} %get-tuple-element.259, s32[32]{0:T(128)S(1)} %get-tuple-element.234, f32[32,128,512]{2,1,0:T(8,128)} %broadcast_multiply_fusion.5), kind=kCustom, calls=%fused_computation.2.clone.1 | custom fusion | flops 2097152 | bytes 25165952 | tf_op jit(solution)/shard_map/while/body/scatter-add | solution.py:39
  134.9 4.4 gather_fusion
  139.3 7.0 %broadcast_multiply_fusion.5 = f32[32,128,512]{2,1,0:T(8,128)} fusion(f32[32]{0:T(128)S(1)} %compare_convert_fusion.3, bf16[32,128,512]{2,1,0:T(8,128)(2,1)} %gather_fusion, bf16[256,128,128]{2,1,0:T(8,128)(2,1)} %get-tuple-element.274, s32[]{:T(128)S(6)} %select_n.44), kind=kOutput, calls=%fused_computation.4.clone.1 | convolution fusion | flops 538968064 | bytes 13631620 | tf_op jit(solution)/shard_map/while/body/tij,tjf->tif/dot_general | solution.py:36
  146.3 11.8 %scatter_fusion = f32[8,128,512]{2,1,0:T(8,128)S(1)} fusion(f32[8,128,512]{2,1,0:T(8,128)S(1)} %get-tuple-element.259, s32[32]{0:T(128)S(1)} %get-tuple-element.234, f32[32,128,512]{2,1,0:T(8,128)} %broadcast_multiply_fusion.5), kind=kCustom, calls=%fused_computation.2.clone.1 | custom fusion | flops 2097152 | bytes 25165952 | tf_op jit(solution)/shard_map/while/body/scatter-add | solution.py:39
  158.1 87.7 %all-reduce.7 = bf16[1024,512]{1,0:T(8,128)(2,1)} all-reduce(f32[1024,512]{1,0:T(8,128)S(1)} %bitcast.16), channel_id=1, replica_groups=mesh['node'=8,'rep'=4] {'rep'}, use_global_device_ids=true, to_apply=%region_3.4 | all-reduce | flops 524288 | bytes 3145728 | tf_op jit(solution)/shard_map/psum | solution.py:63
  245.8 5.3 fusion.6
  254.2 121.5 %all-reduce.4.cloned.1.call-done = f32[512,512]{1,0:T(8,128)} async-done(((f32[512,512]{1,0:T(8,128)}), f32[512,512]{1,0:T(8,128)}) %all-reduce.4.cloned.1.call-update) | async-done | bytes 1048592 | tf_op jit(solution)/shard_map/psum | solution.py:74
  378.3 117.3 %while.21 = (s32[]{:T(128)}, f32[16,128,512]{2,1,0:T(8,128)}, s32[]{:T(128)}, s32[256]{0:T(256)S(1)}, bf16[256,128,128]{2,1,0:T(8,128)(2,1)}, /*index=5*/s32[256...) while((s32[]{:T(128)}, f32[16,128,512]{2,1,0:T(8,128)}, ...), condition=%wide.region_8.9_spmd, body=%wide.region_6.8_spmd.sunk | while | flops 541066688 | bytes 47191480 | solution.py:41
  379.1 2.8 gather_fusion.1
  381.9 7.5 %broadcast_multiply_fusion.6 = f32[32,128,512]{2,1,0:T(8,128)} fusion(f32[32]{0:T(128)S(1)} %and_select_fusion.2, bf16[32,128,512]{2,1,0:T(8,128)(2,1)} %gather_fusion.1, bf16[256,128,128]{2,1,0:T(8,128)(2,1)} %get-tuple-element.310, s32[]{:T(128)S(6)} %select_n.46), kind=kOutput, calls=%fused_computation.11.clone.1 | convolution fusion | flops 538968064 | bytes 13631620 | tf_op jit(solution)/shard_map/while/body/tji,tjf->tif/dot_general | solution.py:32
  389.4 18.6 %scatter_fusion.1 = f32[16,128,512]{2,1,0:T(8,128)} fusion(f32[16,128,512]{2,1,0:T(8,128)} %get-tuple-element.295, s32[32]{0:T(128)S(1)} %get-tuple-element.244, f32[32,128,512]{2,1,0:T(8,128)} %broadcast_multiply_fusion.6), kind=kCustom, calls=%fused_computation.3.clone.1 | custom fusion | flops 2097152 | bytes 25165952 | tf_op jit(solution)/shard_map/while/body/scatter-add | solution.py:35
  408.7 2.8 gather_fusion.1
  411.5 7.3 %broadcast_multiply_fusion.6 = f32[32,128,512]{2,1,0:T(8,128)} fusion(f32[32]{0:T(128)S(1)} %and_select_fusion.2, bf16[32,128,512]{2,1,0:T(8,128)(2,1)} %gather_fusion.1, bf16[256,128,128]{2,1,0:T(8,128)(2,1)} %get-tuple-element.310, s32[]{:T(128)S(6)} %select_n.46), kind=kOutput, calls=%fused_computation.11.clone.1 | convolution fusion | flops 538968064 | bytes 13631620 | tf_op jit(solution)/shard_map/while/body/tji,tjf->tif/dot_general | solution.py:32
  418.8 18.5 %scatter_fusion.1 = f32[16,128,512]{2,1,0:T(8,128)} fusion(f32[16,128,512]{2,1,0:T(8,128)} %get-tuple-element.295, s32[32]{0:T(128)S(1)} %get-tuple-element.244, f32[32,128,512]{2,1,0:T(8,128)} %broadcast_multiply_fusion.6), kind=kCustom, calls=%fused_computation.3.clone.1 | custom fusion | flops 2097152 | bytes 25165952 | tf_op jit(solution)/shard_map/while/body/scatter-add | solution.py:35
  438.1 2.8 gather_fusion.1
  440.9 7.3 %broadcast_multiply_fusion.6 = f32[32,128,512]{2,1,0:T(8,128)} fusion(f32[32]{0:T(128)S(1)} %and_select_fusion.2, bf16[32,128,512]{2,1,0:T(8,128)(2,1)} %gather_fusion.1, bf16[256,128,128]{2,1,0:T(8,128)(2,1)} %get-tuple-element.310, s32[]{:T(128)S(6)} %select_n.46), kind=kOutput, calls=%fused_computation.11.clone.1 | convolution fusion | flops 538968064 | bytes 13631620 | tf_op jit(solution)/shard_map/while/body/tji,tjf->tif/dot_general | solution.py:32
  448.2 18.2 %scatter_fusion.1 = f32[16,128,512]{2,1,0:T(8,128)} fusion(f32[16,128,512]{2,1,0:T(8,128)} %get-tuple-element.295, s32[32]{0:T(128)S(1)} %get-tuple-element.244, f32[32,128,512]{2,1,0:T(8,128)} %broadcast_multiply_fusion.6), kind=kCustom, calls=%fused_computation.3.clone.1 | custom fusion | flops 2097152 | bytes 25165952 | tf_op jit(solution)/shard_map/while/body/scatter-add | solution.py:35
  467.2 2.8 gather_fusion.1
  469.9 7.3 %broadcast_multiply_fusion.6 = f32[32,128,512]{2,1,0:T(8,128)} fusion(f32[32]{0:T(128)S(1)} %and_select_fusion.2, bf16[32,128,512]{2,1,0:T(8,128)(2,1)} %gather_fusion.1, bf16[256,128,128]{2,1,0:T(8,128)(2,1)} %get-tuple-element.310, s32[]{:T(128)S(6)} %select_n.46), kind=kOutput, calls=%fused_computation.11.clone.1 | convolution fusion | flops 538968064 | bytes 13631620 | tf_op jit(solution)/shard_map/while/body/tji,tjf->tif/dot_general | solution.py:32
  477.2 18.5 %scatter_fusion.1 = f32[16,128,512]{2,1,0:T(8,128)} fusion(f32[16,128,512]{2,1,0:T(8,128)} %get-tuple-element.295, s32[32]{0:T(128)S(1)} %get-tuple-element.244, f32[32,128,512]{2,1,0:T(8,128)} %broadcast_multiply_fusion.6), kind=kCustom, calls=%fused_computation.3.clone.1 | custom fusion | flops 2097152 | bytes 25165952 | tf_op jit(solution)/shard_map/while/body/scatter-add | solution.py:35
  495.7 3.8 convert_element_type.37
  503.8 176.0 %reduce-scatter.2.cloned.1.call-done = bf16[256,512]{1,0:T(8,128)(2,1)} async-done(((bf16[2048,512]{1,0:T(8,128)(2,1)}), bf16[256,512]{1,0:T(8,128)(2,1)}) %reduce-scatter.2.cloned.1.call-update) | async-done | bytes 262160 | tf_op jit(solution)/shard_map/reduce_scatter | solution.py:79
  (48 shorter events, 17.8 us)
Async XLA Ops:
  7.2 238.7 %copy-start = (bf16[512,512]{1,0:T(8,128)(2,1)S(1)}, bf16[512,512]{1,0:T(8,128)(2,1)}, u32[]{:S(2)}) copy-start(bf16[512,512]{1,0:T(8,128)(2,1)} %param.12) | copy-start | bytes 1572868
  7.2 55.1 %copy-start.1 = (s32[256]{0:T(256)S(1)}, s32[256]{0:T(256)}, u32[]{:S(2)}) copy-start(s32[256]{0:T(256)} %param.16) | copy-start | bytes 3076
  7.2 55.1 %copy-start.2 = (s32[256]{0:T(256)S(1)}, s32[256]{0:T(256)}, u32[]{:S(2)}) copy-start(s32[256]{0:T(256)} %param.15) | copy-start | bytes 3076
  7.2 54.8 %all-gather.3.cloned.1.call-start = ((), (), s32[]{:S(2)}) async-start(), calls=%async_computation.1 | async-start | bytes 2359296 | tf_op jit(solution)/shard_map/all_gather | solution.py:50
  7.9 237.9 %all-gather.5.cloned.1.call-start = ((), (), s32[]{:S(2)}) async-start(), calls=%async_computation.2 | async-start | bytes 1310720 | tf_op jit(solution)/shard_map/all_gather | solution.py:64
  8.7 367.1 %all-reduce.4.cloned.1.call-start = ((), (), s32[]{:S(2)}) async-start(), calls=%async_computation.3 | async-start | bytes 2097152 | tf_op jit(solution)/shard_map/psum | solution.py:74
  253.4 248.1 %all-reduce.6.cloned.1.call-start = ((), (), s32[]{:S(2)}) async-start(), calls=%async_computation.4 | async-start | bytes 2097152 | tf_op jit(solution)/shard_map/psum | solution.py:74
  375.8 304.0 %reduce-scatter.2.cloned.1.call-start = ((), (), s32[]{:S(2)}) async-start(), calls=%async_computation.5 | async-start | bytes 2359296 | tf_op jit(solution)/shard_map/reduce_scatter | solution.py:79
Sparse Core Ops, SparseCore 0:
  10.1 51.7 all-gather.2
  63.5 15.2 all-gather.4
  253.6 122.1 all-reduce.3
  378.0 35.8 all-reduce.5
  499.6 180.1 reduce-scatter.1
